TPU v7x, 128 devices: a whole 4x4x4 slice. The times are simulated.
128 devices in a mesh: leaf: 2 (over core), front: 64 (over z, y, x).
Axes of the slice: x: 4, y: 4, z: 4, core: 2. Of those that a mesh axis runs over, the one named last changes fastest.
Arguments:
- front_block: float32 [8192, 8192], P('leaf', 'front'), as said below
- child_update: float32 [2, 6144, 8192], P('leaf', None, 'front'), as said below
- child_map: int32 [2, 48], P('leaf'), may hold values from 0 to 63, as said below
Outputs:
- factored: float32 [8192, 8192], P('leaf', 'front')
Inputs may be any that keep to these rules, and one draw needn't show every extreme that they name: `child_map`: each row is strictly increasing, holds 48 distinct blocks, and always names block 0 and block 63. `front_block`: Symmetric; the assembled front is positive definite. `child_update`: each child's update is symmetric and positive semidefinite in the child's order; columns of parent blocks that the child's map does not name are zero.
All inputs are finite; a program needn't handle non-finite values.
Results may differ from a plain program's by a relative error of at most 0.000088.
Values sent between devices are 32-bit elements; how exact they have to be, the bound alone decides.
A program may use at most 128 MiB of HBM per device.

v0:
```python
import jax
import jax.numpy as jnp
from jax import lax
from jax.sharding import PartitionSpec as P

BLK = 128
S = 512
HIGHEST = lax.Precision.HIGHEST


def gather_half(blocks, child_map, half, half_blocks):
    parent = half * half_blocks + jnp.arange(half_blocks, dtype=jnp.int32)
    hit = child_map[None, :] == parent[:, None]
    found = jnp.any(hit, axis=1)
    index = jnp.argmax(hit, axis=1)
    picked = jnp.take(blocks, index, axis=0)
    picked = jnp.where(found[:, None, None], picked, jnp.zeros_like(picked))
    return picked.reshape(half_blocks * BLK, blocks.shape[2])


def per_device(front_block, child_update, child_map):
    rows, cols = front_block.shape
    n_leaf = lax.axis_size("leaf")
    n_front = lax.axis_size("front")
    leaf = lax.axis_index("leaf")
    front = lax.axis_index("front")
    half_blocks = rows // BLK
    blocks = child_update[0].reshape(-1, BLK, cols)
    cmap = child_map[0]
    own = gather_half(blocks, cmap, leaf, half_blocks)
    send = gather_half(blocks, cmap, 1 - leaf, half_blocks)
    recv = lax.ppermute(send, "leaf", [(0, 1), (1, 0)])
    first = jnp.where(leaf == 0, own, recv)
    second = jnp.where(leaf == 0, recv, own)
    assembled = front_block + first + second
    top = assembled[:S]
    piv_cols = S // cols
    is_piv = front < piv_cols
    col_at = jnp.minimum(front, piv_cols - 1) * cols
    panel = lax.dynamic_update_slice_in_dim(
        jnp.zeros((S, S), jnp.float32), jnp.where(is_piv, top, jnp.zeros_like(top)), col_at, 1
    )
    pivot = lax.psum(panel, "front")
    factor = jnp.linalg.cholesky(pivot)
    own_solved = lax.linalg.triangular_solve(factor, top, left_side=True, lower=True).T
    from_leaf0 = lax.ppermute(own_solved, "leaf", [(0, 1)])
    col_solved = jnp.where(leaf == 0, own_solved, from_leaf0)
    piece = rows // n_front
    per_block = BLK // piece
    pieces = []
    for part in range(per_block):
        pairs = []
        for lf in range(n_leaf):
            for k in range(n_front // per_block):
                src = lf * n_front + lf * half_blocks + k
                dst = lf * n_front + per_block * k + part
                pairs.append((src, dst))
        pieces.append(
            lax.ppermute(col_solved[part * piece : (part + 1) * piece], ("leaf", "front"), pairs)
        )
    my_piece = pieces[0]
    for part in range(1, per_block):
        my_piece = jnp.where(front % per_block == part, pieces[part], my_piece)
    row_solved = lax.all_gather(my_piece, "front", tiled=True)
    schur = assembled - jnp.dot(row_solved, col_solved.T, precision=HIGHEST)
    row_global = leaf * rows + jnp.arange(rows, dtype=jnp.int32)
    col_global = front * cols + jnp.arange(cols, dtype=jnp.int32)
    col_start = jnp.minimum(front * cols, S - cols)
    left_rows = lax.dynamic_slice_in_dim(row_solved, col_start, cols, 1)
    left_top = jnp.pad(
        lax.dynamic_slice_in_dim(factor, col_start, cols, 1), ((0, rows - S), (0, 0))
    )
    left_part = jnp.where(row_global[:, None] < S, left_top, left_rows)
    right_top = jnp.pad(col_solved.T, ((0, rows - S), (0, 0)))
    right_part = jnp.where(row_global[:, None] < S, right_top, schur)
    return jnp.where(col_global[None, :] < S, left_part, right_part)


def solution(mesh):
    return jax.shard_map(
        per_device,
        mesh=mesh,
        in_specs=(P("leaf", "front"), P("leaf", None, "front"), P("leaf", None)),
        out_specs=P("leaf", "front"),
        check_vma=False,
    )
```

profile of v0, /device:TPU:1, one launch (start us, length us, event | category | flops | bytes accessed | tf_op | source)
XLA Modules:
  0.0 471.3 jit_solution(12014427817205239228)
XLA Ops:
  12.3 3.2 select_select_fusion
  15.5 2.9 copy.84
  21.8 3.2 select_select_fusion.1
  25.1 2.9 copy.83
  28.0 2.9 copy.56
  30.8 3.3 select_add_fusion
  37.1 129.3 %all-reduce.5.cloned.1.call-done = f32[512,512]{0,1:T(8,128)} async-done(((f32[512,512]{0,1:T(8,128)}), f32[512,512]{0,1:T(8,128)}) %all-reduce.5.cloned.1.call-update) | async-done | bytes 1048592 | tf_op jit(solution)/shard_map/psum | solution.py:43
  166.4 2.6 copy.57
  171.8 11.7 %cholesky.103 = f32[128,128]{1,0:T(8,128)S(1)} custom-call(f32[128,128]{1,0:T(8,128)S(1)} %cholesky.263), custom_call_target="Cholesky" | custom-call | tf_op jit(solution)/shard_map/jit(cholesky)/cholesky | solution.py:44
  184.3 9.8 %custom-call.30 = f32[1,128,128]{1,2,0:T(8,128)S(1)} custom-call(f32[1,128,128]{2,1,0:T(8,128)S(1)} %get-tuple-element.55), custom_call_target="InvertDiagBlocksLowerTriangular" | custom-call | tf_op jit(solution)/shard_map/jit(cholesky)/cholesky | solution.py:44
  198.9 13.2 %cholesky.215 = f32[128,128]{1,0:T(8,128)} custom-call(f32[128,128]{1,0:T(8,128)} %cholesky.267), custom_call_target="Cholesky" | custom-call | tf_op jit(solution)/shard_map/jit(cholesky)/cholesky | solution.py:44
  215.1 11.4 %custom-call.31 = f32[1,128,128]{1,2,0:T(8,128)} custom-call(f32[1,128,128]{2,1,0:T(8,128)} %get-tuple-element.53), custom_call_target="InvertDiagBlocksLowerTriangular" | custom-call | tf_op jit(solution)/shard_map/jit(cholesky)/cholesky | solution.py:44
  232.1 11.7 %cholesky.236 = f32[128,128]{1,0:T(8,128)S(1)} custom-call(f32[128,128]{1,0:T(8,128)S(1)} %cholesky.272), custom_call_target="Cholesky" | custom-call | tf_op jit(solution)/shard_map/jit(cholesky)/cholesky | solution.py:44
  244.6 9.8 %custom-call.32 = f32[1,128,128]{1,2,0:T(8,128)S(1)} custom-call(f32[1,128,128]{2,1,0:T(8,128)S(1)} %get-tuple-element.51), custom_call_target="InvertDiagBlocksLowerTriangular" | custom-call | tf_op jit(solution)/shard_map/jit(cholesky)/cholesky | solution.py:44
  256.8 11.9 %cholesky.253 = f32[128,128]{1,0:T(8,128)S(1)} custom-call(f32[128,128]{1,0:T(8,128)S(1)} %convolution_subtract_fusion.3), custom_call_target="Cholesky" | custom-call | tf_op jit(solution)/shard_map/jit(cholesky)/cholesky | solution.py:44
  276.3 14.5 %while.1 = (s32[]{:T(128)}, f32[512,512]{0,1:T(8,128)}, s32[4,2]{0,1:T(2,128)S(1)}, f32[4,128,128]{2,1,0:T(8,128)}, s32[]{:T(128)}) while((s32[]{:T(128)}, f32[512,512]{0,1:T(8,128)}, s32[4,2]{0,1:T(2,128)S(1)}, f32[4,128,128]{2,1,0:T(8,128)}, s32[]{:T(128)}) %tuple.35), condition=%wide.while_cond, body=%wide.while_body.sunk | while | flops 2 | bytes 393329 | solution.py:45
  290.8 40.1 %custom-call.33 = f32[4,128,128]{1,2,0:T(8,128)S(1)} custom-call(f32[4,128,128]{2,1,0:T(8,128)} %get-tuple-element.17), custom_call_target="InvertDiagBlocksLowerTriangular" | custom-call | tf_op jit(solution)/shard_map/triangular_solve | solution.py:45
  342.4 4.9 %collective-permute-done.1 = f32[128,512]{1,0:T(8,128)S(1)} collective-permute-done((f32[128,512]{1,0:T(8,128)S(1)}, f32[128,512]{1,0:T(8,128)S(1)}, u32[]{:S(2)}, u32[]{:S(2)}) %collective-permute-start.1) | collective-permute-done | bytes 262176 | tf_op jit(solution)/shard_map/ppermute | solution.py:46
  351.4 4.8 %collective-permute-done.3 = f32[64,512]{1,0:T(8,128)S(1)} collective-permute-done((f32[64,512]{1,0:T(8,128)}, f32[64,512]{1,0:T(8,128)S(1)}, u32[]{:S(2)}, u32[]{:S(2)}) %collective-permute-start.3) | collective-permute-done | bytes 131104 | tf_op jit(solution)/shard_map/ppermute | solution.py:59
  358.7 80.8 %all-gather.2.cloned.1.call-done = f32[4096,512]{1,0:T(8,128)} async-done(((f32[64,512]{1,0:T(8,128)}), f32[4096,512]{1,0:T(8,128)}) %all-gather.2.cloned.1.call-update) | async-done | bytes 8388624 | tf_op jit(solution)/shard_map/all_gather | solution.py:64
  439.5 4.2 constant_dynamic-slice_fusion.1
  443.7 2.9 copy.86
  446.6 14.8 %select_select_fusion.2 = f32[4096,128]{0,1:T(8,128)} fusion(f32[512,128]{0,1:T(8,128)S(1)} %bitcast.58, f32[4096,128]{0,1:T(8,128)} %copy.86, f32[512,128]{0,1:T(8,128)} %constant_dynamic-slice_fusion.2, pred[128]{0:T(512)(128)(4,1)S(1)} %add_compare_fusion.1, pred[4096]{0:T(1024)(128)(4,1)S(1)} %add_compare_fusion, f32[4096,128]{0,1:T(8,128)} %copy-done.1, ...), kind=kOutput, calls=%fused_computation.7 | convolution fusion | flops 3223322624 | bytes 15470720 | tf_op jit(solution)/shard_map/dot_general | solution.py:65
  461.4 2.9 copy.75
  (106 shorter events, 69.6 us)
Async XLA Ops:
  6.5 3.8 copy-start
  6.5 159.9 %all-reduce.5.cloned.1.call-start = ((), (), s32[]{:S(2)}) async-start(), calls=%async_computation | async-start | bytes 2097152 | tf_op jit(solution)/shard_map/psum | solution.py:43
  18.4 12.4 %collective-permute-start = (f32[4096,128]{0,1:T(8,128)}, f32[4096,128]{0,1:T(8,128)}, u32[]{:S(2)}, u32[]{:S(2)}) collective-permute-start(f32[4096,128]{0,1:T(8,128)} %copy.84), channel_id=1, source_target_pairs={{0,64},{64,0},{1,65},{65,1},{2,66},{66,2},{3,67},{67,3},{4,68},{68... | collective-permute-start | bytes 6291464 | tf_op jit(solution)/shard_map/ppermute | solution.py:32
  34.1 1.7 copy-start.1
  36.6 403.0 %all-gather.2.cloned.1.call-start = ((), (), s32[]{:S(2)}) async-start(), calls=%async_computation.1 | async-start | bytes 8519680 | tf_op jit(solution)/shard_map/all_gather | solution.py:64
  170.8 1.0 copy-start.3
  197.4 31.0 %copy-start.4 = (f32[384,128]{1,0:T(8,128)S(1)}, f32[384,128]{1,0:T(8,128)}, u32[]{:S(2)}) copy-start(f32[384,128]{1,0:T(8,128)} %convolution_subtract_fusion.1) | copy-start | bytes 589828
  229.5 1.0 copy-start.2
  331.0 0.7 copy-start.6
  339.9 2.5 copy-start.5
  341.1 6.2 %collective-permute-start.1 = (f32[128,512]{1,0:T(8,128)S(1)}, f32[128,512]{1,0:T(8,128)S(1)}, u32[]{:S(2)}, u32[]{:S(2)}) collective-permute-start(f32[128,512]{1,0:T(8,128)S(1)} %maximum_bitcast_fusion), channel_id=1, source_target_pairs={{0,64},{1,65},{2,66},{3,67},{4,68},{5,69},{6,70},{7,71},{8,72},{9,... | collective-permute-start | bytes 786440 | tf_op jit(solution)/shard_map/ppermute | solution.py:46
  348.8 7.4 %collective-permute-start.3 = (f32[64,512]{1,0:T(8,128)}, f32[64,512]{1,0:T(8,128)S(1)}, u32[]{:S(2)}, u32[]{:S(2)}) collective-permute-start(f32[64,512]{1,0:T(8,128)} %get-tuple-element.48), channel_id=1, source_target_pairs={{0,0},{1,2},{2,4},{3,6},{4,8},{5,10},{6,12},{7,14},{8,16},{9,18},{... | collective-permute-start | bytes 393224 | tf_op jit(solution)/shard_map/ppermute | solution.py:59
  350.1 6.1 %collective-permute-start.2 = (f32[64,512]{1,0:T(8,128)}, f32[64,512]{1,0:T(8,128)}, u32[]{:S(2)}, u32[]{:S(2)}) collective-permute-start(f32[64,512]{1,0:T(8,128)} %get-tuple-element.49), channel_id=1, source_target_pairs={{0,1},{1,3},{2,5},{3,7},{4,9},{5,11},{6,13},{7,15},{8,17},{9,19},{... | collective-permute-start | bytes 393224 | tf_op jit(solution)/shard_map/ppermute | solution.py:59
Sparse Core Ops, SparseCore 0:
  36.7 129.7 all-reduce.4
  357.1 82.4 all-gather.1
where the time goes:
time: 476 us; the launch traced here: 471 us
  waiting for transfers between devices  220 us (46%)
  other arithmetic  143 us (30%)
  local copies, waits for them, and re-layouts  54 us (11%)
  matrix products  32.1 us (7%)
  between operations  16.5 us (3%)
  starting transfers between devices  5.81 us (1%)
    psum x1, waiting for transfers between devices, per_device(): pivot = lax.psum(panel, 'front')  129 us
    another operation x15, other arithmetic, per_device(): factor = jnp.linalg.cholesky(pivot)  83.8 us
    all_gather x1, waiting for transfers between devices, per_device(): row_solved = lax.all_gather(my_piece, 'front', tiled=True)  80.8 us
    another operation x3, other arithmetic, per_device(): lax.linalg.triangular_solve(factor, top, left_side=True, lower=True)  41.7 us
    dot_general x1, matrix products, per_device(): schur = assembled - jnp.dot(row_solved, col_solved.T, precision=HIGHEST)  14.8 us
    another operation x20, local copies, waits for them, and re-layouts  14.5 us
  transfers between devices with their start and end apart: 6, of which 4 were waited for; matrix products, arithmetic and copies ran while one was open for 3% of the time, Pallas kernels for 0%

commit v1 on v0

--- a/solution.py
+++ b/solution.py
@@ -40,7 +40,7 @@
     panel = lax.dynamic_update_slice_in_dim(
         jnp.zeros((S, S), jnp.float32), jnp.where(is_piv, top, jnp.zeros_like(top)), col_at, 1
     )
-    pivot = lax.psum(panel, "front")
+    pivot = jnp.sum(lax.all_gather(panel, "front"), axis=0)
     factor = jnp.linalg.cholesky(pivot)
     own_solved = lax.linalg.triangular_solve(factor, top, left_side=True, lower=True).T
     from_leaf0 = lax.ppermute(own_solved, "leaf", [(0, 1)])

time: 476 us -> 608 us (1.28)
  waiting for transfers between devices: 220 us -> 369 us
  local copies, waits for them, and re-layouts: 54 us -> 29 us
  other arithmetic: 143 us -> 160 us
    all_gather x0 -> x1, waiting for transfers between devices: none -> 279 us  [per_device(): pivot = jnp.sum(lax.all_gather(panel, 'front'), axis=0)]
    psum x1 -> x0, waiting for transfers between devices: 129 us -> none  [per_device(): pivot = lax.psum(panel, 'front')]
    reduce_sum x0 -> x1, other arithmetic: none -> 22 us  [per_device(): pivot = jnp.sum(lax.all_gather(panel, 'front'), axis=0)]
    unnamed x16 -> x8, local copies, waits for them, and re-layouts: 8.79 us -> 1.51 us
    another operation x20 -> x12, local copies, waits for them, and re-layouts: 14.5 us -> 14.1 us
  transfers between devices with their start and end apart: 6 -> 6, of which waited for: 4 -> 5; matrix products, arithmetic and copies ran while one was open for 3% -> 1% of each run, Pallas kernels for 0% -> 0%
where the time goes in v1:
time: 608 us; the launch traced here: 607 us
  waiting for transfers between devices  369 us (61%)
  other arithmetic  160 us (26%)
  local copies, waits for them, and re-layouts  29 us (5%)
  matrix products  26.9 us (4%)
  between operations  16.2 us (3%)
    all_gather x1, waiting for transfers between devices, per_device(): pivot = jnp.sum(lax.all_gather(panel, 'front'), axis=0)  279 us
    another operation x15, other arithmetic, per_device(): factor = jnp.linalg.cholesky(pivot)  81.1 us
    all_gather x1, waiting for transfers between devices, per_device(): row_solved = lax.all_gather(my_piece, 'front', tiled=True)  77.4 us
    another operation x3, other arithmetic, per_device(): lax.linalg.triangular_solve(factor, top, left_side=True, lower=True)  42 us
    reduce_sum x1, other arithmetic, per_device(): pivot = jnp.sum(lax.all_gather(panel, 'front'), axis=0)  22 us
    another operation x12, local copies, waits for them, and re-layouts  14.1 us
  transfers between devices with their start and end apart: 6, of which 5 were waited for; matrix products, arithmetic and copies ran while one was open for 1% of the time, Pallas kernels for 0%

profile of v1, /device:TPU:1, one launch (start us, length us, event | category | flops | bytes accessed | tf_op | source)
XLA Modules:
  0.0 606.6 jit_solution(4179081448976312932)
XLA Ops:
  10.3 2.0 gather_fusion.1
  12.3 3.2 select_select_fusion
  16.9 2.0 gather_fusion
  18.9 2.0 select_select_fusion.1
  25.5 278.8 %all-gather.3.cloned.1.call-done = f32[64,512,512]{2,1,0:T(8,128)} async-done(((f32[1,512,512]{2,1,0:T(8,128)}), f32[64,512,512]{2,1,0:T(8,128)}) %all-gather.3.cloned.1.call-update) | async-done | bytes 67108880 | tf_op jit(solution)/shard_map/all_gather | solution.py:43
  304.3 22.0 %reduce_sum.9 = f32[512,512]{1,0:T(8,128)} reduce(f32[64,512,512]{2,1,0:T(8,128)} %all-gather.3.cloned.1.call-done, f32[]{:T(128)} %constant.191.clone.1), dimensions={0}, to_apply=%region_4.6 | reduce | flops 16515072 | bytes 68157440 | tf_op jit(solution)/shard_map/reduce_sum | solution.py:43
  326.3 2.5 copy.8
  331.6 11.7 %cholesky.103 = f32[128,128]{1,0:T(8,128)S(1)} custom-call(f32[128,128]{1,0:T(8,128)S(1)} %cholesky.263), custom_call_target="Cholesky" | custom-call | tf_op jit(solution)/shard_map/jit(cholesky)/cholesky | solution.py:44
  344.5 9.8 %custom-call.30 = f32[1,128,128]{1,2,0:T(8,128)S(1)} custom-call(f32[1,128,128]{2,1,0:T(8,128)S(1)} %get-tuple-element.43), custom_call_target="InvertDiagBlocksLowerTriangular" | custom-call | tf_op jit(solution)/shard_map/jit(cholesky)/cholesky | solution.py:44
  357.5 11.7 %cholesky.215 = f32[128,128]{1,0:T(8,128)S(1)} custom-call(f32[128,128]{1,0:T(8,128)S(1)} %cholesky.267), custom_call_target="Cholesky" | custom-call | tf_op jit(solution)/shard_map/jit(cholesky)/cholesky | solution.py:44
  371.2 10.0 %custom-call.31 = f32[1,128,128]{1,2,0:T(8,128)S(1)} custom-call(f32[1,128,128]{2,1,0:T(8,128)S(1)} %get-tuple-element.40), custom_call_target="InvertDiagBlocksLowerTriangular" | custom-call | tf_op jit(solution)/shard_map/jit(cholesky)/cholesky | solution.py:44
  383.6 11.7 %cholesky.236 = f32[128,128]{1,0:T(8,128)S(1)} custom-call(f32[128,128]{1,0:T(8,128)S(1)} %cholesky.272), custom_call_target="Cholesky" | custom-call | tf_op jit(solution)/shard_map/jit(cholesky)/cholesky | solution.py:44
  396.6 9.8 %custom-call.32 = f32[1,128,128]{1,2,0:T(8,128)S(1)} custom-call(f32[1,128,128]{2,1,0:T(8,128)S(1)} %get-tuple-element.37), custom_call_target="InvertDiagBlocksLowerTriangular" | custom-call | tf_op jit(solution)/shard_map/jit(cholesky)/cholesky | solution.py:44
  408.7 11.7 %cholesky.253 = f32[128,128]{1,0:T(8,128)S(1)} custom-call(f32[128,128]{1,0:T(8,128)S(1)} %convolution_subtract_fusion.3), custom_call_target="Cholesky" | custom-call | tf_op jit(solution)/shard_map/jit(cholesky)/cholesky | solution.py:44
  426.1 14.1 %while.1 = (s32[]{:T(128)}, f32[512,512]{1,0:T(8,128)}, s32[4,2]{0,1:T(2,128)S(1)}, f32[4,128,128]{2,1,0:T(8,128)}, s32[]{:T(128)}) while((s32[]{:T(128)}, f32[512,512]{1,0:T(8,128)}, s32[4,2]{0,1:T(2,128)S(1)}, f32[4,128,128]{2,1,0:T(8,128)}, s32[]{:T(128)}) %tuple.34), condition=%wide.while_cond, body=%wide.while_body.sunk | while | flops 2 | bytes 132705 | solution.py:45
  426.8 2.9 bitcast_dynamic-update-slice_fusion.2
  430.4 2.9 bitcast_dynamic-update-slice_fusion.2
  433.9 2.9 bitcast_dynamic-update-slice_fusion.2
  437.4 2.8 bitcast_dynamic-update-slice_fusion.2
  440.2 40.1 %custom-call.33 = f32[4,128,128]{1,2,0:T(8,128)S(1)} custom-call(f32[4,128,128]{2,1,0:T(8,128)} %get-tuple-element.17), custom_call_target="InvertDiagBlocksLowerTriangular" | custom-call | tf_op jit(solution)/shard_map/triangular_solve | solution.py:45
  489.7 2.9 collective-permute-done.1
  496.2 9.8 %collective-permute-done.3 = f32[64,512]{0,1:T(8,128)} collective-permute-done((f32[64,512]{0,1:T(8,128)}, f32[64,512]{0,1:T(8,128)}, u32[]{:S(2)}, u32[]{:S(2)}) %collective-permute-start.3) | collective-permute-done | bytes 131104 | tf_op jit(solution)/shard_map/ppermute | solution.py:59
  511.3 77.4 %all-gather.5.cloned.1.call-done = f32[4096,512]{1,0:T(8,128)} async-done(((f32[64,512]{1,0:T(8,128)}), f32[4096,512]{1,0:T(8,128)}) %all-gather.5.cloned.1.call-update) | async-done | bytes 8388624 | tf_op jit(solution)/shard_map/all_gather | solution.py:64
  588.7 11.1 %select_select_fusion.2 = f32[4096,128]{1,0:T(8,128)} fusion(f32[512,128]{1,0:T(8,128)S(1)} %bitcast.70, f32[4096,512]{1,0:T(8,128)} %all-gather.5.cloned.1.call-done, s32[]{:T(128)S(6)} %select_n.94, f32[512,128]{1,0:T(8,128)} %constant_dynamic-slice_fusion.1, pred[4096]{0:T(1024)(128)(4,1)S(1)} %add_compare_fusion, ...), kind=kOutput, calls=%fused_computation.11 | convolution fusion | flops 3223322624 | bytes 15470724 | tf_op jit(solution)/shard_map/dot_general | solution.py:65
  (77 shorter events, 48.8 us)
Async XLA Ops:
  6.5 3.8 copy-start
  6.5 297.7 %all-gather.3.cloned.1.call-start = ((), (), s32[]{:S(2)}) async-start(), calls=%async_computation | async-start | bytes 68157440 | tf_op jit(solution)/shard_map/all_gather | solution.py:43
  15.5 5.6 collective-permute-start
  18.9 2.2 copy-start.3
  23.0 1.7 copy-start.1
  25.4 563.3 %all-gather.5.cloned.1.call-start = ((), (), s32[]{:S(2)}) async-start(), calls=%async_computation.1 | async-start | bytes 8519680 | tf_op jit(solution)/shard_map/all_gather | solution.py:64
  330.6 1.0 copy-start.2
  488.4 4.2 collective-permute-start.1
  493.5 2.7 collective-permute-start.2
  494.9 11.1 %collective-permute-start.3 = (f32[64,512]{0,1:T(8,128)}, f32[64,512]{0,1:T(8,128)}, u32[]{:S(2)}, u32[]{:S(2)}) collective-permute-start(f32[64,512]{0,1:T(8,128)} %get-tuple-element.32), channel_id=1, source_target_pairs={{0,0},{1,2},{2,4},{3,6},{4,8},{5,10},{6,12},{7,14},{8,16},{9,18},{... | collective-permute-start | bytes 393224 | tf_op jit(solution)/shard_map/ppermute | solution.py:59
Sparse Core Ops, SparseCore 0:
  25.6 278.6 all-gather.2
  509.5 79.1 all-gather.4
